TPU v7x, 32 devices: a whole 2x2x4 slice. The times are simulated.
32 devices in a mesh: sweep: 2 (over y), tm: 4 (over z), height: 2 (over x), width: 2 (over core).
Axes of the slice: x: 2, y: 2, z: 4, core: 2. Of those that a mesh axis runs over, the one named last changes fastest.
Arguments:
- queries: bfloat16 [8, 2, 4, 64, 2560], P(('sweep', 'tm'), 'height', 'width'), parts along dimension 0, may hold values from -8 to 8
- keys: bfloat16 [8, 2, 4, 64, 2560], P(('sweep', 'tm'), 'height', 'width'), parts along dimension 0, may hold values from -8 to 8
- values: bfloat16 [8, 2, 4, 64, 2560], P(('sweep', 'tm'), 'height', 'width'), parts along dimension 0, may hold values from -6 to 6
- windows: int32 [20, 3], replicated, may hold values from 0 to 1, as said below
- tile_mask: int32 [4, 2, 4, 27], P('tm', 'height', 'width'), may hold values 0 or 1
- coefficient: float32 [2], P('sweep'), parts along dimension 0, may hold values from 0.5 to 1.5
- layer: int32 [2], P('sweep'), parts along dimension 0, may hold values from 0 to 39
- steering: bfloat16 [40, 2560], replicated, may hold values from -4 to 4
Outputs:
- attended: bfloat16 [8, 2, 4, 64, 2560], P(('sweep', 'tm'), 'height', 'width'), parts along dimension 0
There are 2 independent parts, one for each index of `sweep`. A program takes and returns all parts, laid end to end along the dimension named above; an argument that names none is the same for every part. Nothing has to cross between parts.
Inputs may be any that keep to these rules, and one draw needn't show every extreme that they name: `windows`: some head reaches one tile along all three dimensions.
All inputs are finite; a program needn't handle non-finite values. No bound on the sum of `tile_mask` on one device may be relied on, other than what follows from the above.
Results may differ from a plain program's by a relative error of at most 0.0045.
Values may be sent and summed in bfloat16 or wider, within the bound.
A program may use at most 192 MiB of HBM per device.

v0:
```python
import functools
import math

import jax
import jax.numpy as jnp
from jax import lax
from jax.experimental import pallas as pl
from jax.experimental.pallas import tpu as pltpu
from jax.sharding import PartitionSpec as P

DH = 128
NEG = -1e30
MESH = pl.DeviceIdType.MESH
HC = 2


def kernel(
    n_tm, n_height, heads,
    q_ref, k_ref, v_ref, win_ref, mask_ref, coef_ref, layer_ref, steer_ref,
    out_ref,
    kbuf, vbuf, qbuf, mbuf, bias, scores, svec, ostage,
    ssem, rsem, lsem, qsem, msem, osem,
):
    tokens = q_ref.shape[0]
    cols = mask_ref.shape[0]
    tile = tokens // cols
    all_cols = 2 * cols
    half = (heads // 2) * DH
    cw = HC * DH
    chunks = half // cw
    c = lax.axis_index("width")
    z = lax.axis_index("tm")
    x = lax.axis_index("height")
    sib = 1 - c
    if n_height == 1:
        rows = []
    elif n_height == 2:
        rows = [(1 - 2 * x, True, 1)]
    else:
        rows = [(-1, x > 0, 2), (1, x < n_height - 1, 1)]
    nr = 1 + len(rows)
    ns = 3 * nr
    frames = [(-1, z > 0, 2), (1, z < n_tm - 1, 1)]
    bufs = ((k_ref, kbuf), (v_ref, vbuf))

    def guard(cond, body):
        if cond is True:
            body()
        else:
            pl.when(cond)(body)

    barrier = pltpu.get_barrier_semaphore()

    def greet(**where):
        pl.semaphore_signal(barrier, inc=1, device_id=where, device_id_type=MESH)

    greet(width=sib)
    expect = jnp.int32(1)
    for d, ok, _ in rows:
        def body(d=d):
            for t in range(2):
                greet(height=x + d, width=jnp.int32(t))
        guard(ok, body)
        expect = expect + (2 if ok is True else 2 * ok.astype(jnp.int32))
    for d, ok, _ in frames:
        def body(d=d):
            for t in range(2):
                greet(tm=z + d, width=jnp.int32(t))
        guard(ok, body)
        expect = expect + 2 * ok.astype(jnp.int32)
    pl.semaphore_wait(barrier, expect)

    def remote(src, dst, s, r, where):
        return pltpu.make_async_remote_copy(
            src_ref=src, dst_ref=dst, send_sem=s, recv_sem=r, device_id=where, device_id_type=MESH
        )

    def columns(core, g):
        return pl.ds(pl.multiple_of(core * half + g * cw, DH), cw)

    def own(kv, dest, g, core, slot, where):
        src, buf = bufs[kv]
        return remote(
            src.at[:, columns(core, g)], buf.at[slot, g, c],
            ssem.at[kv, dest, g, core], rsem.at[kv, slot, g, c], where,
        )

    def to_sibling(kv, g):
        return own(kv, 0, g, sib, 0, dict(width=sib))

    def to_row(kv, i, g, core):
        d, _, there = rows[i]
        return own(kv, 1 + i, g, jnp.int32(core), there, dict(height=x + d, width=jnp.int32(core)))

    def to_frame(kv, i, g, core):
        d, _, there = frames[i]
        return own(kv, nr + i, g, jnp.int32(core), there * nr, dict(tm=z + d, width=jnp.int32(core)))

    def forward(kv, j, i, g):
        d, _, there = frames[i]
        buf = bufs[kv][1]
        return remote(
            buf.at[1 + j, g], buf.at[there * nr + 1 + j, g],
            ssem.at[kv, nr + 2 + 2 * j + i, g, 0], rsem.at[kv, there * nr + 1 + j, g, 0],
            dict(tm=z + d),
        )

    def arrived(kv, slot, g, core):
        src, buf = bufs[kv]
        return remote(
            src.at[:, columns(core, g)], buf.at[slot, g, core],
            ssem.at[kv, 0, g, core], rsem.at[kv, slot, g, core], dict(width=sib),
        )

    def forwarded(kv, slot, g):
        buf = bufs[kv][1]
        return remote(
            buf.at[slot, g], buf.at[slot, g],
            ssem.at[kv, 0, g, 0], rsem.at[kv, slot, g, 0], dict(width=sib),
        )

    def keep(kv, g):
        src, buf = bufs[kv]
        return pltpu.make_async_copy(src.at[:, columns(c, g)], buf.at[0, g, c], lsem.at[kv, g])

    def keep_q(g):
        return pltpu.make_async_copy(q_ref.at[:, columns(c, g)], qbuf.at[g, c], lsem.at[2, g])

    def send_q(g):
        return remote(
            q_ref.at[:, columns(sib, g)], qbuf.at[g, c], qsem.at[0, g], qsem.at[1, g], dict(width=sib)
        )

    def send_mask():
        return remote(mask_ref, mbuf, msem.at[0], msem.at[1], dict(width=sib))

    def row_ok(i):
        return rows[i][1]

    send_mask().start()

    def start_rows(g, _):
        for i in range(nr - 1):
            def body(i=i):
                for core in range(2):
                    for kv in range(2):
                        to_row(kv, i, g, core).start()
            guard(row_ok(i), body)
        return 0

    def start_frames(g):
        for i in range(2):
            def body(i=i):
                for core in range(2):
                    for kv in range(2):
                        to_frame(kv, i, g, core).start()
            guard(frames[i][1], body)

    def start_local(g, _):
        keep_q(g).start()
        send_q(g).start()
        for kv in range(2):
            keep(kv, g).start()
            to_sibling(kv, g).start()
        return 0

    start_rows(0, 0)
    start_frames(0)
    lax.fori_loop(1, chunks, start_rows, 0)
    lax.fori_loop(0, chunks, start_local, 0)

    for i in range(nr - 1):
        if row_ok(i) is not True:
            @pl.when(jnp.logical_not(row_ok(i)))
            def _(i=i):
                for f in range(3):
                    for _, buf in bufs:
                        buf[f * nr + 1 + i] = jnp.zeros(buf.shape[1:], buf.dtype)
    for i in range(2):
        @pl.when(jnp.logical_not(frames[i][1]))
        def _(i=i):
            for j in range(nr):
                for _, buf in bufs:
                    def zero(g, _, j=j, buf=buf):
                        buf[(1 + i) * nr + j, g] = jnp.zeros(buf.shape[2:], buf.dtype)
                        return 0
                    if j == 0 or row_ok(j - 1) is True:
                        lax.fori_loop(0, chunks, zero, 0)
                    else:
                        @pl.when(row_ok(j - 1))
                        def _(zero=zero):
                            lax.fori_loop(0, chunks, zero, 0)

    pick = lax.broadcasted_iota(jnp.int32, (steer_ref.shape[0], DH), 0) == layer_ref[0]
    for h in range(heads):
        rows_f32 = steer_ref[:, h * DH : (h + 1) * DH].astype(jnp.float32)
        svec[h] = coef_ref[0] * jnp.sum(jnp.where(pick, rows_f32, 0.0), axis=0, keepdims=True)

    def pump(g, _):
        @pl.when(g > 0)
        def _():
            start_frames(g)
        for j in range(nr - 1):
            def body(j=j):
                for core in range(2):
                    for kv in range(2):
                        arrived(kv, 1 + j, g, jnp.int32(core)).wait_recv()
                for i in range(2):
                    def inner(i=i):
                        for kv in range(2):
                            forward(kv, j, i, g).start()
                    guard(frames[i][1], inner)
            guard(row_ok(j), body)
        return 0

    lax.fori_loop(0, chunks, pump, 0)

    send_mask().wait_recv()
    theirs = mbuf[...]
    mine = mask_ref[...]
    first = jnp.where(c == 0, mine, theirs)
    second = jnp.where(c == 0, theirs, mine)
    kept = jnp.concatenate([first, second], axis=0)
    span = all_cols * tile
    lane = lax.broadcasted_iota(jnp.int32, (1, kept.shape[1]), 1)
    block = lax.broadcasted_iota(jnp.int32, (1, span), 1) // tile
    for f in range(3):
        df = (0, -1, 1)[f]
        f_ok = True if f == 0 else frames[f - 1][1]
        for r in range(nr):
            dr = 0 if r == 0 else rows[r - 1][0]
            r_ok = True if r == 0 else row_ok(r - 1)
            base = 9 * (df + 1) + 3 * (dr + 1)
            slot = f * nr + r
            ok = None
            for cond in (f_ok, r_ok):
                if cond is not True:
                    ok = cond if ok is None else jnp.logical_and(ok, cond)
            for qc in range(all_cols):
                line = jnp.full((1, span), NEG, jnp.float32)
                for kc in range(max(qc - 1, 0), min(qc + 2, all_cols)):
                    if slot == 0 and kc == qc:
                        value = jnp.zeros((1, 1), jnp.float32)
                    else:
                        here = jnp.where(lane == base + (kc - qc + 1), kept[qc : qc + 1], 0)
                        hit = jnp.sum(here.astype(jnp.float32), axis=1, keepdims=True)
                        value = jnp.where(hit == 1.0, 0.0, NEG)
                        if ok is not None:
                            value = jnp.where(ok, value, NEG)
                    line = jnp.where(block == kc, value, line)
                alone = jnp.where(block == qc, line, NEG)
                at = pl.ds(qc * tile, tile)
                bias[slot, at, :] = jnp.broadcast_to(alone, (tile, span))
                bias[ns + slot, at, :] = jnp.broadcast_to(line, (tile, span))
    bias[2 * ns] = jnp.full((span, span), NEG, jnp.float32)

    scale = 1.0 / math.sqrt(DH)

    def out_home(g):
        return pltpu.make_async_copy(
            ostage.at[g, c], out_ref.at[:, columns(c, g)], lsem.at[3, g]
        )

    def out_away(g):
        return remote(
            ostage.at[g, sib], out_ref.at[:, columns(c, g)], osem.at[0, g], osem.at[1, g], dict(width=sib)
        )

    def out_arrived(g):
        return remote(
            ostage.at[g, sib], out_ref.at[:, columns(sib, g)], osem.at[0, g], osem.at[1, g], dict(width=sib)
        )

    def attend(g, _):
        keep_q(g).wait()
        send_q(g).wait_recv()
        for kv in range(2):
            keep(kv, g).wait()
            arrived(kv, 0, g, sib).wait_recv()
        for i in range(2):
            def body(i=i):
                for kv in range(2):
                    for core in range(2):
                        arrived(kv, (1 + i) * nr, g, jnp.int32(core)).wait_recv()
                    for j in range(nr - 1):
                        def inner(j=j, kv=kv):
                            forwarded(kv, (1 + i) * nr + 1 + j, g).wait_recv()
                        guard(row_ok(j), inner)
            guard(frames[i][1], body)
        for hh in range(HC):
            h = c * (heads // 2) + g * HC + hh
            lanes = slice(hh * DH, (hh + 1) * DH)
            wf, wr, wc = win_ref[h, 0], win_ref[h, 1], win_ref[h, 2]
            q = qbuf[g][:, :, lanes].reshape(span, DH)
            top = None
            for slot in range(ns):
                index = jnp.where(wc >= 1, ns + slot, slot)
                if slot // nr > 0:
                    index = jnp.where(wf >= 1, index, 2 * ns)
                if slot % nr > 0:
                    index = jnp.where(wr >= 1, index, 2 * ns)
                key = kbuf[slot, g][:, :, lanes].reshape(span, DH)
                s = lax.dot_general(
                    q, key, (((1,), (1,)), ((), ())), preferred_element_type=jnp.float32
                )
                s = s * scale + bias[index]
                scores[slot] = s
                high = jnp.maximum(s[:, :DH], s[:, DH:]) if span == 2 * DH else jnp.max(s, axis=1, keepdims=True)
                top = high if top is None else jnp.maximum(top, high)
            top = jnp.max(top, axis=1, keepdims=True)
            total = None
            mixture = None
            for slot in range(ns):
                e = jnp.exp(scores[slot] - top)
                part = e[:, :DH] + e[:, DH:] if span == 2 * DH else jnp.sum(e, axis=1, keepdims=True)
                total = part if total is None else total + part
                value = vbuf[slot, g][:, :, lanes].reshape(span, DH)
                term = jnp.dot(e.astype(jnp.bfloat16), value, preferred_element_type=jnp.float32)
                mixture = term if mixture is None else mixture + term
            total = jnp.sum(total, axis=1, keepdims=True)
            attended = mixture * (1.0 / total) + svec[h]
            ostage[g, :, :, lanes] = attended.astype(ostage.dtype).reshape(2, tokens, DH)
        out_home(g).start()
        out_away(g).start()
        return 0

    lax.fori_loop(0, chunks, attend, 0)

    send_mask().wait_send()

    def drain(g, _):
        send_q(g).wait_send()
        for kv in range(2):
            to_sibling(kv, g).wait_send()
        for i in range(nr - 1):
            def body(i=i):
                for core in range(2):
                    for kv in range(2):
                        to_row(kv, i, g, core).wait_send()
            guard(row_ok(i), body)
        for i in range(2):
            def body(i=i):
                for kv in range(2):
                    for core in range(2):
                        to_frame(kv, i, g, core).wait_send()
                    for j in range(nr - 1):
                        def inner(j=j, kv=kv):
                            forward(kv, j, i, g).wait_send()
                        guard(row_ok(j), inner)
            guard(frames[i][1], body)
        out_home(g).wait()
        out_away(g).wait_send()
        out_arrived(g).wait_recv()
        return 0

    lax.fori_loop(0, chunks, drain, 0)


def solution(mesh):
    n_tm, n_height = mesh.shape["tm"], mesh.shape["height"]

    def per_device(queries, keys, values, windows, tile_mask, coefficient, layer, steering):
        frames, rows, cols, tile, features = queries.shape
        heads = features // DH
        tokens = frames * rows * cols * tile
        chunks = heads // 2 // HC
        cw = HC * DH
        span = 2 * tokens
        nr = min(n_height, 3)
        ns = 3 * nr
        flat = (tokens, features)
        hbm = pl.BlockSpec(memory_space=pl.ANY)
        vmem = pl.BlockSpec(memory_space=pltpu.VMEM)
        smem = pl.BlockSpec(memory_space=pltpu.SMEM)
        bf16 = jnp.bfloat16
        out = pl.pallas_call(
            functools.partial(kernel, n_tm, n_height, heads),
            out_shape=jax.ShapeDtypeStruct(flat, bf16),
            in_specs=[hbm, hbm, hbm, smem, vmem, smem, smem, vmem],
            out_specs=hbm,
            scratch_shapes=[
                pltpu.VMEM((ns, chunks, 2, tokens, cw), bf16),
                pltpu.VMEM((ns, chunks, 2, tokens, cw), bf16),
                pltpu.VMEM((chunks, 2, tokens, cw), bf16),
                pltpu.VMEM((cols, tile_mask.shape[-1]), jnp.int32),
                pltpu.VMEM((2 * ns + 1, span, span), jnp.float32),
                pltpu.VMEM((ns, span, span), jnp.float32),
                pltpu.VMEM((heads, 1, DH), jnp.float32),
                pltpu.VMEM((chunks, 2, tokens, cw), bf16),
                pltpu.SemaphoreType.DMA((2, 3 * nr, chunks, 2)),
                pltpu.SemaphoreType.DMA((2, ns, chunks, 2)),
                pltpu.SemaphoreType.DMA((4, chunks)),
                pltpu.SemaphoreType.DMA((2, chunks)),
                pltpu.SemaphoreType.DMA((2,)),
                pltpu.SemaphoreType.DMA((2, chunks)),
            ],
            compiler_params=pltpu.CompilerParams(
                collective_id=0, has_side_effects=True, vmem_limit_bytes=48 * 1024 * 1024
            ),
        )(
            queries.reshape(flat), keys.reshape(flat), values.reshape(flat), windows,
            tile_mask.reshape(cols, tile_mask.shape[-1]), coefficient, layer, steering,
        )
        return out.reshape(queries.shape)

    tiles = P(("sweep", "tm"), "height", "width", None, None)
    return jax.shard_map(
        per_device,
        mesh=mesh,
        in_specs=(tiles, tiles, tiles, P(), P("tm", "height", "width", None), P("sweep"), P("sweep"), P()),
        out_specs=tiles,
        check_vma=False,
    )
```

profile of v0, /device:TPU:0, one launch (start us, length us, event | category | flops | bytes accessed | tf_op | source)
XLA Modules:
  0.0 75.6 jit_solution(10144434878059341376)
XLA Ops:
  1.3 0.0 copy-start.5
  1.3 0.7 copy-done.5
  2.0 0.0 copy-start.4
  2.0 0.1 copy.9.win_ref
  2.1 0.6 copy-done.4
  2.7 0.0 copy-start
  2.7 1.1 %copy-done = bf16[1,1,2,64,2560]{4,3,2,1,0:T(8,128)(2,1)S(1)} copy-done((bf16[1,1,2,64,2560]{4,3,2,1,0:T(8,128)(2,1)S(1)}, bf16[1,1,2,64,2560]{4,3,2,1,0:T(8,128)(2,1)}, u32[]{:S(2)}) %copy-start) | copy-done | bytes 655384
  3.7 0.0 copy-start.1
  3.8 1.1 %copy-done.1 = bf16[1,1,2,64,2560]{4,3,2,1,0:T(8,128)(2,1)S(1)} copy-done((bf16[1,1,2,64,2560]{4,3,2,1,0:T(8,128)(2,1)S(1)}, bf16[1,1,2,64,2560]{4,3,2,1,0:T(8,128)(2,1)}, u32[]{:S(2)}) %copy-start.1) | copy-done | bytes 655384
  4.8 0.0 copy-start.2
  4.8 1.1 %copy-done.2 = bf16[1,1,2,64,2560]{4,3,2,1,0:T(8,128)(2,1)S(1)} copy-done((bf16[1,1,2,64,2560]{4,3,2,1,0:T(8,128)(2,1)S(1)}, bf16[1,1,2,64,2560]{4,3,2,1,0:T(8,128)(2,1)}, u32[]{:S(2)}) %copy-start.2) | copy-done | bytes 655384
  5.9 0.0 copy-start.3
  5.9 0.9 %copy-done.3 = bf16[40,2560]{1,0:T(8,128)(2,1)S(1)} copy-done((bf16[40,2560]{1,0:T(8,128)(2,1)S(1)}, bf16[40,2560]{1,0:T(8,128)(2,1)}, u32[]{:S(2)}) %copy-start.3) | copy-done | bytes 204824
  6.9 67.9 %shard_map.82 = bf16[128,2560]{1,0:T(8,128)(2,1)S(1)} custom-call(bf16[128,2560]{1,0:T(8,128)(2,1)S(1)} %bitcast.6, bf16[128,2560]{1,0:T(8,128)(2,1)S(1)} %bitcast.7, bf16[128,2560]{1,0:T(8,128)(2,1)S(1)} %bitcast.8, s32[20,3]{1,0:T(8,128)S(1)} %copy.9.win_ref, s32[2,27]{1,0:T(2,128)S(1)} %bitcast.9, f32[1]{0:T(128)S(6)} %copy.11.coef_ref, ...), custom_call_target="tpu_custom_call" | custom-call | tf_op jit(solution)/shard_map/pallas_call | solution.py:376
  74.8 0.8 %copy.13 = bf16[1,1,2,64,2560]{4,3,2,1,0:T(8,128)(2,1)} copy(bf16[1,1,2,64,2560]{4,3,2,1,0:T(8,128)(2,1)S(1)} %bitcast.5) | data formatting | bytes 1310720
Async XLA Ops:
  1.3 0.7 copy-start.5
  2.0 0.7 copy-start.4
  2.7 1.1 %copy-start = (bf16[1,1,2,64,2560]{4,3,2,1,0:T(8,128)(2,1)S(1)}, bf16[1,1,2,64,2560]{4,3,2,1,0:T(8,128)(2,1)}, u32[]{:S(2)}) copy-start(bf16[1,1,2,64,2560]{4,3,2,1,0:T(8,128)(2,1)} %param.8) | copy-start | bytes 1966084
  3.7 1.1 %copy-start.1 = (bf16[1,1,2,64,2560]{4,3,2,1,0:T(8,128)(2,1)S(1)}, bf16[1,1,2,64,2560]{4,3,2,1,0:T(8,128)(2,1)}, u32[]{:S(2)}) copy-start(bf16[1,1,2,64,2560]{4,3,2,1,0:T(8,128)(2,1)} %param.9) | copy-start | bytes 1966084
  4.8 1.1 %copy-start.2 = (bf16[1,1,2,64,2560]{4,3,2,1,0:T(8,128)(2,1)S(1)}, bf16[1,1,2,64,2560]{4,3,2,1,0:T(8,128)(2,1)}, u32[]{:S(2)}) copy-start(bf16[1,1,2,64,2560]{4,3,2,1,0:T(8,128)(2,1)} %param.10) | copy-start | bytes 1966084
  5.9 0.9 %copy-start.3 = (bf16[40,2560]{1,0:T(8,128)(2,1)S(1)}, bf16[40,2560]{1,0:T(8,128)(2,1)}, u32[]{:S(2)}) copy-start(bf16[40,2560]{1,0:T(8,128)(2,1)} %steer_ref.1) | copy-start | bytes 614404
where the time goes:
time: 76 us; the launch traced here: 75.6 us
  Pallas kernels  67.9 us (89%)
  local copies, waits for them, and re-layouts  6.38 us (8%)
  between operations  1.32 us (2%)
    pallas_call x1, Pallas kernels, per_device(): pl.pallas_call(functools.partial(kernel, n_tm, n_height, heads), out_shap...  67.9 us
    unnamed x14, local copies, waits for them, and re-layouts  6.38 us

commit v1 on v0

--- a/solution.py
+++ b/solution.py
@@ -15,13 +15,14 @@
 
 
 def kernel(
-    n_tm, n_height, heads,
-    q_ref, k_ref, v_ref, win_ref, mask_ref, coef_ref, layer_ref, steer_ref,
+    n_tm, n_height, heads, reach_chunks,
+    q_hbm, k_hbm, v_hbm, win_ref, mask_hbm, coef_ref, layer_ref, steer_hbm,
     out_ref,
     kbuf, vbuf, qbuf, mbuf, bias, scores, svec, ostage,
-    ssem, rsem, lsem, qsem, msem, osem,
+    raw, byhead, q_ref, k_ref, v_ref, owhole, mask_ref, steer_ref, rank, perm,
+    ssem, rsem, lsem, qsem, msem, osem, isem,
 ):
-    tokens = q_ref.shape[0]
+    tokens = raw.shape[1]
     cols = mask_ref.shape[0]
     tile = tokens // cols
     all_cols = 2 * cols
@@ -49,6 +50,15 @@
         else:
             pl.when(cond)(body)
 
+    loads = [
+        pltpu.make_async_copy(src, raw.at[i], isem.at[i])
+        for i, src in enumerate((k_hbm, v_hbm, q_hbm))
+    ]
+    loads.append(pltpu.make_async_copy(mask_hbm, mask_ref, isem.at[3]))
+    loads.append(pltpu.make_async_copy(steer_hbm, steer_ref, isem.at[4]))
+    for load in loads:
+        load.start()
+
     barrier = pltpu.get_barrier_semaphore()
 
     def greet(**where):
@@ -68,6 +78,40 @@
                 greet(tm=z + d, width=jnp.int32(t))
         guard(ok, body)
         expect = expect + 2 * ok.astype(jnp.int32)
+
+    reaching = jnp.int32(0)
+    flags = [jnp.where(win_ref[0, h] >= 1, 1, 0) for h in range(heads)]
+    for h in range(heads):
+        rank[h] = reaching
+        reaching = reaching + flags[h]
+    for h in range(heads):
+        rank[h] = jnp.where(flags[h] == 1, rank[h], reaching + h - rank[h])
+
+    def invert(i, _):
+        head = jnp.int32(0)
+        for h in range(heads):
+            head = jnp.where(rank[h] == i, h, head)
+        perm[i] = head
+        return 0
+
+    lax.fori_loop(0, heads, invert, 0)
+
+    def pack(which, ref):
+        loads[which].wait()
+        for h in range(heads):
+            byhead[which, h] = raw[which, :, h * DH : (h + 1) * DH]
+
+        def one(g, _):
+            for core in range(2):
+                for hh in range(HC):
+                    head = perm[(g * HC + hh) * 2 + core]
+                    ref[g, core, :, hh * DH : (hh + 1) * DH] = byhead[which, head]
+            return 0
+
+        lax.fori_loop(0, chunks, one, 0)
+
+    pack(0, k_ref)
+    pack(1, v_ref)
     pl.semaphore_wait(barrier, expect)
 
     def remote(src, dst, s, r, where):
@@ -75,13 +119,10 @@
             src_ref=src, dst_ref=dst, send_sem=s, recv_sem=r, device_id=where, device_id_type=MESH
         )
 
-    def columns(core, g):
-        return pl.ds(pl.multiple_of(core * half + g * cw, DH), cw)
-
     def own(kv, dest, g, core, slot, where):
         src, buf = bufs[kv]
         return remote(
-            src.at[:, columns(core, g)], buf.at[slot, g, c],
+            src.at[g, core], buf.at[slot, g, c],
             ssem.at[kv, dest, g, core], rsem.at[kv, slot, g, c], where,
         )
 
@@ -108,7 +149,7 @@
     def arrived(kv, slot, g, core):
         src, buf = bufs[kv]
         return remote(
-            src.at[:, columns(core, g)], buf.at[slot, g, core],
+            src.at[g, core], buf.at[slot, g, core],
             ssem.at[kv, 0, g, core], rsem.at[kv, slot, g, core], dict(width=sib),
         )
 
@@ -121,18 +162,18 @@
 
     def keep(kv, g):
         src, buf = bufs[kv]
-        return pltpu.make_async_copy(src.at[:, columns(c, g)], buf.at[0, g, c], lsem.at[kv, g])
+        return pltpu.make_async_copy(src.at[g, c], buf.at[0, g, c], lsem.at[kv, g])
 
     def keep_q(g):
-        return pltpu.make_async_copy(q_ref.at[:, columns(c, g)], qbuf.at[g, c], lsem.at[2, g])
+        return pltpu.make_async_copy(q_ref.at[g, c], qbuf.at[g, c], lsem.at[2, g])
 
     def send_q(g):
         return remote(
-            q_ref.at[:, columns(sib, g)], qbuf.at[g, c], qsem.at[0, g], qsem.at[1, g], dict(width=sib)
+            q_ref.at[g, sib], qbuf.at[g, c], qsem.at[0, g], qsem.at[1, g], dict(width=sib)
         )
 
     def send_mask():
-        return remote(mask_ref, mbuf, msem.at[0], msem.at[1], dict(width=sib))
+        return remote(mask_hbm, mbuf, msem.at[0], msem.at[1], dict(width=sib))
 
     def row_ok(i):
         return rows[i][1]
@@ -167,7 +208,10 @@
     start_rows(0, 0)
     start_frames(0)
     lax.fori_loop(1, chunks, start_rows, 0)
+    pack(2, q_ref)
     lax.fori_loop(0, chunks, start_local, 0)
+    loads[3].wait()
+    loads[4].wait()
 
     for i in range(nr - 1):
         if row_ok(i) is not True:
@@ -185,11 +229,11 @@
                         buf[(1 + i) * nr + j, g] = jnp.zeros(buf.shape[2:], buf.dtype)
                         return 0
                     if j == 0 or row_ok(j - 1) is True:
-                        lax.fori_loop(0, chunks, zero, 0)
+                        lax.fori_loop(0, reach_chunks, zero, 0)
                     else:
                         @pl.when(row_ok(j - 1))
                         def _(zero=zero):
-                            lax.fori_loop(0, chunks, zero, 0)
+                            lax.fori_loop(0, reach_chunks, zero, 0)
 
     pick = lax.broadcasted_iota(jnp.int32, (steer_ref.shape[0], DH), 0) == layer_ref[0]
     for h in range(heads):
@@ -213,7 +257,7 @@
             guard(row_ok(j), body)
         return 0
 
-    lax.fori_loop(0, chunks, pump, 0)
+    lax.fori_loop(0, reach_chunks, pump, 0)
 
     send_mask().wait_recv()
     theirs = mbuf[...]
@@ -256,28 +300,36 @@
 
     scale = 1.0 / math.sqrt(DH)
 
+    def place(core, g):
+        return owhole.at[core, pl.ds(g * HC, HC)]
+
     def out_home(g):
-        return pltpu.make_async_copy(
-            ostage.at[g, c], out_ref.at[:, columns(c, g)], lsem.at[3, g]
-        )
+        return pltpu.make_async_copy(ostage.at[g, c], place(c, g), lsem.at[3, g])
 
     def out_away(g):
         return remote(
-            ostage.at[g, sib], out_ref.at[:, columns(c, g)], osem.at[0, g], osem.at[1, g], dict(width=sib)
+            ostage.at[g, sib], place(c, g), osem.at[0, g], osem.at[1, g], dict(width=sib)
         )
 
     def out_arrived(g):
         return remote(
-            ostage.at[g, sib], out_ref.at[:, columns(sib, g)], osem.at[0, g], osem.at[1, g], dict(width=sib)
-        )
-
-    def attend(g, _):
+            ostage.at[g, sib], place(sib, g), osem.at[0, g], osem.at[1, g], dict(width=sib)
+        )
+
+    def attend(far, g, _):
         keep_q(g).wait()
         send_q(g).wait_recv()
         for kv in range(2):
             keep(kv, g).wait()
             arrived(kv, 0, g, sib).wait_recv()
-        for i in range(2):
+        if not far:
+            for j in range(nr - 1):
+                def near(j=j):
+                    for core in range(2):
+                        for kv in range(2):
+                            arrived(kv, 1 + j, g, jnp.int32(core)).wait_recv()
+                guard(row_ok(j), near)
+        for i in range(2 if far else 0):
             def body(i=i):
                 for kv in range(2):
                     for core in range(2):
@@ -288,12 +340,12 @@
                         guard(row_ok(j), inner)
             guard(frames[i][1], body)
         for hh in range(HC):
-            h = c * (heads // 2) + g * HC + hh
+            h = perm[(g * HC + hh) * 2 + c]
             lanes = slice(hh * DH, (hh + 1) * DH)
-            wf, wr, wc = win_ref[h, 0], win_ref[h, 1], win_ref[h, 2]
+            wf, wr, wc = win_ref[0, h], win_ref[1, h], win_ref[2, h]
             q = qbuf[g][:, :, lanes].reshape(span, DH)
             top = None
-            for slot in range(ns):
+            for slot in range(ns if far else nr):
                 index = jnp.where(wc >= 1, ns + slot, slot)
                 if slot // nr > 0:
                     index = jnp.where(wf >= 1, index, 2 * ns)
@@ -310,7 +362,7 @@
             top = jnp.max(top, axis=1, keepdims=True)
             total = None
             mixture = None
-            for slot in range(ns):
+            for slot in range(ns if far else nr):
                 e = jnp.exp(scores[slot] - top)
                 part = e[:, :DH] + e[:, DH:] if span == 2 * DH else jnp.sum(e, axis=1, keepdims=True)
                 total = part if total is None else total + part
@@ -319,16 +371,22 @@
                 mixture = term if mixture is None else mixture + term
             total = jnp.sum(total, axis=1, keepdims=True)
             attended = mixture * (1.0 / total) + svec[h]
-            ostage[g, :, :, lanes] = attended.astype(ostage.dtype).reshape(2, tokens, DH)
+            attended = attended.astype(ostage.dtype)
+            ostage[g, 0, hh] = attended[:tokens]
+            ostage[g, 1, hh] = attended[tokens:]
         out_home(g).start()
         out_away(g).start()
         return 0
 
-    lax.fori_loop(0, chunks, attend, 0)
+    last = reach_chunks - 1
+    lax.fori_loop(0, last, functools.partial(attend, True), 0)
+    if reach_chunks < chunks:
+        lax.fori_loop(reach_chunks, chunks, functools.partial(attend, False), 0)
+    lax.fori_loop(last, reach_chunks, functools.partial(attend, True), 0)
 
     send_mask().wait_send()
 
-    def drain(g, _):
+    def drain(far, g, _):
         send_q(g).wait_send()
         for kv in range(2):
             to_sibling(kv, g).wait_send()
@@ -338,7 +396,7 @@
                     for kv in range(2):
                         to_row(kv, i, g, core).wait_send()
             guard(row_ok(i), body)
-        for i in range(2):
+        for i in range(2 if far else 0):
             def body(i=i):
                 for kv in range(2):
                     for core in range(2):
@@ -353,7 +411,13 @@
         out_arrived(g).wait_recv()
         return 0
 
-    lax.fori_loop(0, chunks, drain, 0)
+    lax.fori_loop(0, reach_chunks, functools.partial(drain, True), 0)
+    if reach_chunks < chunks:
+        lax.fori_loop(reach_chunks, chunks, functools.partial(drain, False), 0)
+
+    for h in range(heads):
+        spot = rank[h]
+        out_ref[:, h * DH : (h + 1) * DH] = owhole[spot & 1, spot >> 1]
 
 
 def solution(mesh):
@@ -369,37 +433,59 @@
         nr = min(n_height, 3)
         ns = 3 * nr
         flat = (tokens, features)
-        hbm = pl.BlockSpec(memory_space=pl.ANY)
+        hbm = pl.BlockSpec(memory_space=pltpu.MemorySpace.HBM)
         vmem = pl.BlockSpec(memory_space=pltpu.VMEM)
         smem = pl.BlockSpec(memory_space=pltpu.SMEM)
         bf16 = jnp.bfloat16
-        out = pl.pallas_call(
-            functools.partial(kernel, n_tm, n_height, heads),
-            out_shape=jax.ShapeDtypeStruct(flat, bf16),
-            in_specs=[hbm, hbm, hbm, smem, vmem, smem, smem, vmem],
-            out_specs=hbm,
-            scratch_shapes=[
-                pltpu.VMEM((ns, chunks, 2, tokens, cw), bf16),
-                pltpu.VMEM((ns, chunks, 2, tokens, cw), bf16),
-                pltpu.VMEM((chunks, 2, tokens, cw), bf16),
-                pltpu.VMEM((cols, tile_mask.shape[-1]), jnp.int32),
-                pltpu.VMEM((2 * ns + 1, span, span), jnp.float32),
-                pltpu.VMEM((ns, span, span), jnp.float32),
-                pltpu.VMEM((heads, 1, DH), jnp.float32),
-                pltpu.VMEM((chunks, 2, tokens, cw), bf16),
-                pltpu.SemaphoreType.DMA((2, 3 * nr, chunks, 2)),
-                pltpu.SemaphoreType.DMA((2, ns, chunks, 2)),
-                pltpu.SemaphoreType.DMA((4, chunks)),
-                pltpu.SemaphoreType.DMA((2, chunks)),
-                pltpu.SemaphoreType.DMA((2,)),
-                pltpu.SemaphoreType.DMA((2, chunks)),
-            ],
-            compiler_params=pltpu.CompilerParams(
-                collective_id=0, has_side_effects=True, vmem_limit_bytes=48 * 1024 * 1024
-            ),
-        )(
-            queries.reshape(flat), keys.reshape(flat), values.reshape(flat), windows,
-            tile_mask.reshape(cols, tile_mask.shape[-1]), coefficient, layer, steering,
+        offsets = tile_mask.shape[-1]
+        packed = pltpu.VMEM((chunks, 2, tokens, cw), bf16)
+
+        def attention(number, reach_chunks):
+            return pl.pallas_call(
+                functools.partial(kernel, n_tm, n_height, heads, reach_chunks),
+                out_shape=jax.ShapeDtypeStruct(flat, bf16),
+                in_specs=[hbm, hbm, hbm, smem, hbm, smem, smem, hbm],
+                out_specs=vmem,
+                scratch_shapes=[
+                    pltpu.VMEM((ns, chunks, 2, tokens, cw), bf16),
+                    pltpu.VMEM((ns, chunks, 2, tokens, cw), bf16),
+                    packed,
+                    pltpu.VMEM((cols, offsets), jnp.int32),
+                    pltpu.VMEM((2 * ns + 1, span, span), jnp.float32),
+                    pltpu.VMEM((ns, span, span), jnp.float32),
+                    pltpu.VMEM((heads, 1, DH), jnp.float32),
+                    pltpu.VMEM((chunks, 2, HC, tokens, DH), bf16),
+                    pltpu.VMEM((3, tokens, features), bf16),
+                    pltpu.VMEM((3, heads, tokens, DH), bf16),
+                    packed,
+                    packed,
+                    packed,
+                    pltpu.VMEM((2, chunks * HC, tokens, DH), bf16),
+                    pltpu.VMEM((cols, offsets), jnp.int32),
+                    pltpu.VMEM(steering.shape, bf16),
+                    pltpu.SMEM((heads,), jnp.int32),
+                    pltpu.SMEM((heads,), jnp.int32),
+                    pltpu.SemaphoreType.DMA((2, 3 * nr, chunks, 2)),
+                    pltpu.SemaphoreType.DMA((2, ns, chunks, 2)),
+                    pltpu.SemaphoreType.DMA((4, chunks)),
+                    pltpu.SemaphoreType.DMA((2, chunks)),
+                    pltpu.SemaphoreType.DMA((2,)),
+                    pltpu.SemaphoreType.DMA((2, chunks)),
+                    pltpu.SemaphoreType.DMA((5,)),
+                ],
+                compiler_params=pltpu.CompilerParams(
+                    collective_id=number, has_side_effects=True, vmem_limit_bytes=48 * 1024 * 1024
+                ),
+            )
+
+        least = 2
+        reaching = jnp.sum((windows[:, 0] >= 1).astype(jnp.int32))
+        needed = sum((reaching > 2 * HC * n).astype(jnp.int32) for n in range(least, chunks))
+        out = lax.switch(
+            needed,
+            [attention(n, least + n) for n in range(chunks - least + 1)],
+            queries.reshape(flat), keys.reshape(flat), values.reshape(flat), windows.T,
+            tile_mask.reshape(cols, offsets), coefficient, layer, steering,
         )
         return out.reshape(queries.shape)
 

time: 76 us -> 52.1 us (0.69)
  Pallas kernels: 67.9 us -> 46.9 us
  local copies, waits for them, and re-layouts: 6.38 us -> 1.52 us
  other arithmetic: 0 us -> 1.32 us
    pallas_call x1, Pallas kernels: 67.9 us -> 46.9 us  [per_device(): lax.switch(needed, [attention(n, least + n) for n in range(chunks - least...]
    unnamed x14 -> x5, local copies, waits for them, and re-layouts: 6.38 us -> 1.52 us
    reduce_sum x0 -> x1, other arithmetic: none -> 1.32 us  [per_device(): reaching = jnp.sum((windows[:, 0] >= 1).astype(jnp.int32))]
where the time goes in v1:
time: 52.1 us; the launch traced here: 51.9 us
  Pallas kernels  46.9 us (90%)
  between operations  1.98 us (4%)
  local copies, waits for them, and re-layouts  1.52 us (3%)
  other arithmetic  1.32 us (3%)
    pallas_call x1, Pallas kernels, per_device(): lax.switch(needed, [attention(n, least + n) for n in range(chunks - least...  46.9 us
    unnamed x5, local copies, waits for them, and re-layouts  1.52 us
    reduce_sum x1, other arithmetic, per_device(): reaching = jnp.sum((windows[:, 0] >= 1).astype(jnp.int32))  1.32 us

profile of v1, /device:TPU:0, one launch (start us, length us, event | category | flops | bytes accessed | tf_op | source)
XLA Modules:
  0.0 51.9 jit_solution(10613861100489077198)
XLA Ops:
  0.0 1.3 %fusion = s32[]{:T(128)} fusion(s32[20,3]{0,1:T(4,128)} %param.15), kind=kLoop, calls=%fused_computation.1 | loop fusion | flops 59 | bytes 84 | tf_op jit(solution)/shard_map/reduce_sum | solution.py:482
  3.3 0.0 copy-start
  3.3 0.0 copy-start.1
  3.3 0.7 %copy-done = s32[20,3]{0,1:T(4,128)S(1)} copy-done((s32[20,3]{0,1:T(4,128)S(1)}, s32[20,3]{0,1:T(4,128)}, u32[]{:S(2)}) %copy-start) | copy-done | bytes 264
  4.0 0.0 copy-done.1
  4.0 47.1 %conditional.1 = (bf16[1,1,2,64,2560]{4,3,2,1,0:T(8,128)(2,1)S(1)}) conditional(s32[]{:T(128)} %clamp.3, (bf16[1,1,2,64,2560]{4,3,2,1,0:T(8,128)(2,1)}, bf16[1,1,2,64,2560]{4,3,2,1,0:T(8,128)(2,1)}, bf16[1,1,2,64,2560]{4,3,2,1,0:T(8,128)(2,1)}, s32[1,1,2,27]{3,2,1,0:T(2,128)S(1)}, s32[3,20]{1,0:T(4,128)S(1)}, ...), branch_computations={%region_1.0_spmd, %region_2.0_spmd, %region_3.0_spmd, %region_4.0_... | conditional | bytes 8 | solution.py:484
  4.0 46.9 %branch_1_fun.1 = bf16[128,2560]{1,0:T(8,128)(2,1)S(1)} custom-call(bf16[128,2560]{1,0:T(8,128)(2,1)} %bitcast.22, bf16[128,2560]{1,0:T(8,128)(2,1)} %bitcast.26, bf16[128,2560]{1,0:T(8,128)(2,1)} %bitcast.30, s32[3,20]{1,0:T(4,128)S(1)} %get-tuple-element.102.win_ref, s32[2,27]{1,0:T(2,128)S(1)} %bitcast.42, f32[1]{0:T(128)} %get-tuple-element.169.coef_ref, ...), custom_call_target="tpu_custom_call" | custom-call | tf_op jit(solution)/shard_map/cond/branch_1_fun/pallas_call | solution.py:484
  51.1 0.8 %copy.46 = bf16[1,1,2,64,2560]{4,3,2,1,0:T(8,128)(2,1)} copy(bf16[1,1,2,64,2560]{4,3,2,1,0:T(8,128)(2,1)S(1)} %get-tuple-element.123) | data formatting | bytes 1310720
Async XLA Ops:
  3.3 0.7 %copy-start = (s32[20,3]{0,1:T(4,128)S(1)}, s32[20,3]{0,1:T(4,128)}, u32[]{:S(2)}) copy-start(s32[20,3]{0,1:T(4,128)} %param.15) | copy-start | bytes 724
  3.3 0.7 %copy-start.1 = (s32[1,1,2,27]{3,2,1,0:T(2,128)S(1)}, s32[1,1,2,27]{3,2,1,0:T(2,128)}, u32[]{:S(2)}) copy-start(s32[1,1,2,27]{3,2,1,0:T(2,128)} %param.16) | copy-start | bytes 652

commit v2 on v1

--- a/solution.py
+++ b/solution.py
@@ -11,11 +11,12 @@
 DH = 128
 NEG = -1e30
 MESH = pl.DeviceIdType.MESH
-HC = 2
+HC = 1
+FULL, CROSS, NEAR = range(3)
 
 
 def kernel(
-    n_tm, n_height, heads, reach_chunks,
+    n_tm, n_height, heads, full_chunks, reach_chunks,
     q_hbm, k_hbm, v_hbm, win_ref, mask_hbm, coef_ref, layer_ref, steer_hbm,
     out_ref,
     kbuf, vbuf, qbuf, mbuf, bias, scores, svec, ostage,
@@ -79,13 +80,18 @@
         guard(ok, body)
         expect = expect + 2 * ok.astype(jnp.int32)
 
-    reaching = jnp.int32(0)
-    flags = [jnp.where(win_ref[0, h] >= 1, 1, 0) for h in range(heads)]
+    along = [jnp.where(win_ref[0, h] >= 1, 1, 0) for h in range(heads)]
+    both = [along[h] * jnp.where(win_ref[1, h] >= 1, 1, 0) for h in range(heads)]
+    n_along = functools.reduce(lambda a, b: a + b, along)
+    n_both = functools.reduce(lambda a, b: a + b, both)
+    place_both, place_along, place_rest = jnp.int32(0), n_both, n_along
     for h in range(heads):
-        rank[h] = reaching
-        reaching = reaching + flags[h]
-    for h in range(heads):
-        rank[h] = jnp.where(flags[h] == 1, rank[h], reaching + h - rank[h])
+        rank[h] = jnp.where(
+            both[h] == 1, place_both, jnp.where(along[h] == 1, place_along, place_rest)
+        )
+        place_both = place_both + both[h]
+        place_along = place_along + along[h] - both[h]
+        place_rest = place_rest + 1 - along[h]
 
     def invert(i, _):
         head = jnp.int32(0)
@@ -228,12 +234,13 @@
                     def zero(g, _, j=j, buf=buf):
                         buf[(1 + i) * nr + j, g] = jnp.zeros(buf.shape[2:], buf.dtype)
                         return 0
+                    count = reach_chunks if j == 0 else full_chunks
                     if j == 0 or row_ok(j - 1) is True:
-                        lax.fori_loop(0, reach_chunks, zero, 0)
+                        lax.fori_loop(0, count, zero, 0)
                     else:
                         @pl.when(row_ok(j - 1))
-                        def _(zero=zero):
-                            lax.fori_loop(0, reach_chunks, zero, 0)
+                        def _(zero=zero, count=count):
+                            lax.fori_loop(0, count, zero, 0)
 
     pick = lax.broadcasted_iota(jnp.int32, (steer_ref.shape[0], DH), 0) == layer_ref[0]
     for h in range(heads):
@@ -257,7 +264,14 @@
             guard(row_ok(j), body)
         return 0
 
-    lax.fori_loop(0, reach_chunks, pump, 0)
+    lax.fori_loop(0, full_chunks, pump, 0)
+
+    def straight(g, _):
+        start_frames(g)
+        return 0
+
+    if full_chunks < reach_chunks:
+        lax.fori_loop(full_chunks, reach_chunks, straight, 0)
 
     send_mask().wait_recv()
     theirs = mbuf[...]
@@ -316,25 +330,29 @@
             ostage.at[g, sib], place(sib, g), osem.at[0, g], osem.at[1, g], dict(width=sib)
         )
 
-    def attend(far, g, _):
+    def attend(kind, g, _):
+        slots = [
+            slot for slot in range(ns)
+            if kind == FULL or slot < nr or (kind == CROSS and slot % nr == 0)
+        ]
         keep_q(g).wait()
         send_q(g).wait_recv()
         for kv in range(2):
             keep(kv, g).wait()
             arrived(kv, 0, g, sib).wait_recv()
-        if not far:
+        if kind != FULL:
             for j in range(nr - 1):
                 def near(j=j):
                     for core in range(2):
                         for kv in range(2):
                             arrived(kv, 1 + j, g, jnp.int32(core)).wait_recv()
                 guard(row_ok(j), near)
-        for i in range(2 if far else 0):
+        for i in range(2 if kind != NEAR else 0):
             def body(i=i):
                 for kv in range(2):
                     for core in range(2):
                         arrived(kv, (1 + i) * nr, g, jnp.int32(core)).wait_recv()
-                    for j in range(nr - 1):
+                    for j in range(nr - 1 if kind == FULL else 0):
                         def inner(j=j, kv=kv):
                             forwarded(kv, (1 + i) * nr + 1 + j, g).wait_recv()
                         guard(row_ok(j), inner)
@@ -345,7 +363,7 @@
             wf, wr, wc = win_ref[0, h], win_ref[1, h], win_ref[2, h]
             q = qbuf[g][:, :, lanes].reshape(span, DH)
             top = None
-            for slot in range(ns if far else nr):
+            for slot in slots:
                 index = jnp.where(wc >= 1, ns + slot, slot)
                 if slot // nr > 0:
                     index = jnp.where(wf >= 1, index, 2 * ns)
@@ -362,7 +380,7 @@
             top = jnp.max(top, axis=1, keepdims=True)
             total = None
             mixture = None
-            for slot in range(ns if far else nr):
+            for slot in slots:
                 e = jnp.exp(scores[slot] - top)
                 part = e[:, :DH] + e[:, DH:] if span == 2 * DH else jnp.sum(e, axis=1, keepdims=True)
                 total = part if total is None else total + part
@@ -378,15 +396,21 @@
         out_away(g).start()
         return 0
 
-    last = reach_chunks - 1
-    lax.fori_loop(0, last, functools.partial(attend, True), 0)
-    if reach_chunks < chunks:
-        lax.fori_loop(reach_chunks, chunks, functools.partial(attend, False), 0)
-    lax.fori_loop(last, reach_chunks, functools.partial(attend, True), 0)
+    def run(start, stop, step, kind):
+        if start < stop:
+            lax.fori_loop(start, stop, functools.partial(step, kind), 0)
+
+    if full_chunks == reach_chunks and 2 * full_chunks > chunks:
+        run(reach_chunks, chunks, attend, NEAR)
+        run(0, full_chunks, attend, FULL)
+    else:
+        run(0, full_chunks, attend, FULL)
+        run(reach_chunks, chunks, attend, NEAR)
+        run(full_chunks, reach_chunks, attend, CROSS)
 
     send_mask().wait_send()
 
-    def drain(far, g, _):
+    def drain(kind, g, _):
         send_q(g).wait_send()
         for kv in range(2):
             to_sibling(kv, g).wait_send()
@@ -396,12 +420,12 @@
                     for kv in range(2):
                         to_row(kv, i, g, core).wait_send()
             guard(row_ok(i), body)
-        for i in range(2 if far else 0):
+        for i in range(2 if kind != NEAR else 0):
             def body(i=i):
                 for kv in range(2):
                     for core in range(2):
                         to_frame(kv, i, g, core).wait_send()
-                    for j in range(nr - 1):
+                    for j in range(nr - 1 if kind == FULL else 0):
                         def inner(j=j, kv=kv):
                             forward(kv, j, i, g).wait_send()
                         guard(row_ok(j), inner)
@@ -411,9 +435,9 @@
         out_arrived(g).wait_recv()
         return 0
 
-    lax.fori_loop(0, reach_chunks, functools.partial(drain, True), 0)
-    if reach_chunks < chunks:
-        lax.fori_loop(reach_chunks, chunks, functools.partial(drain, False), 0)
+    run(0, full_chunks, drain, FULL)
+    run(full_chunks, reach_chunks, drain, CROSS)
+    run(reach_chunks, chunks, drain, NEAR)
 
     for h in range(heads):
         spot = rank[h]
@@ -440,9 +464,9 @@
         offsets = tile_mask.shape[-1]
         packed = pltpu.VMEM((chunks, 2, tokens, cw), bf16)
 
-        def attention(number, reach_chunks):
+        def attention(number, full_chunks, reach_chunks):
             return pl.pallas_call(
-                functools.partial(kernel, n_tm, n_height, heads, reach_chunks),
+                functools.partial(kernel, n_tm, n_height, heads, full_chunks, reach_chunks),
                 out_shape=jax.ShapeDtypeStruct(flat, bf16),
                 in_specs=[hbm, hbm, hbm, smem, hbm, smem, smem, hbm],
                 out_specs=vmem,
@@ -478,12 +502,19 @@
                 ),
             )
 
-        least = 2
-        reaching = jnp.sum((windows[:, 0] >= 1).astype(jnp.int32))
-        needed = sum((reaching > 2 * HC * n).astype(jnp.int32) for n in range(least, chunks))
+        plans = [(5, 5), (4, 6), (4, 7), (6, 6), (5, 8), (7, 7)]
+        plans = [plan for plan in plans if plan[1] < chunks] + [(chunks, chunks)]
+        along = windows[:, 0] >= 1
+        both = along & (windows[:, 1] >= 1)
+        counts = jnp.sum(along.astype(jnp.int32) * 64 + both.astype(jnp.int32))
+        n_along, n_both = counts >> 6, counts & 63
+        choice = jnp.int32(len(plans) - 1)
+        for n, (full, reach) in reversed(list(enumerate(plans[:-1]))):
+            fits = (n_both <= 2 * HC * full) & (n_along <= 2 * HC * reach)
+            choice = jnp.where(fits, n, choice)
         out = lax.switch(
-            needed,
-            [attention(n, least + n) for n in range(chunks - least + 1)],
+            choice,
+            [attention(n, *plan) for n, plan in enumerate(plans)],
             queries.reshape(flat), keys.reshape(flat), values.reshape(flat), windows.T,
             tile_mask.reshape(cols, offsets), coefficient, layer, steering,
         )

time: 52.1 us -> 52 us (level)
  between operations: 1.98 us -> 1.36 us
where the time goes in v2:
time: 52 us; the launch traced here: 51.8 us
  Pallas kernels  47 us (90%)
  local copies, waits for them, and re-layouts  1.52 us (3%)
  other arithmetic  1.4 us (3%)
  between operations  1.36 us (3%)
  loops' own time  0.54 us (1%)
    pallas_call x1, Pallas kernels, per_device(): lax.switch(choice, [attention(n, *plan) for n, plan in enumerate(plans)],...  47 us
    unnamed x5, local copies, waits for them, and re-layouts  1.52 us
    reduce_sum x1, other arithmetic, per_device(): counts = jnp.sum(along.astype(jnp.int32) * 64 + both.astype(jnp.int32))  1.4 us

profile of v2, /device:TPU:0, one launch (start us, length us, event | category | flops | bytes accessed | tf_op | source)
XLA Modules:
  0.0 51.8 jit_solution(4348321045341186127)
XLA Ops:
  0.0 1.4 %fusion.1 = s32[]{:T(128)} fusion(s32[20,3]{0,1:T(4,128)} %param.18), kind=kLoop, calls=%fused_computation.3 | loop fusion | flops 139 | bytes 164 | tf_op jit(solution)/shard_map/reduce_sum | solution.py:509
  2.7 0.0 copy-start
  2.7 0.0 copy-start.1
  2.8 0.7 %copy-done = s32[20,3]{0,1:T(4,128)S(1)} copy-done((s32[20,3]{0,1:T(4,128)S(1)}, s32[20,3]{0,1:T(4,128)}, u32[]{:S(2)}) %copy-start) | copy-done | bytes 264
  3.4 0.0 copy-done.1
  3.4 47.5 %conditional.1 = (bf16[1,1,2,64,2560]{4,3,2,1,0:T(8,128)(2,1)S(1)}) conditional(s32[]{:T(128)} %clamp.3, (bf16[1,1,2,64,2560]{4,3,2,1,0:T(8,128)(2,1)}, bf16[1,1,2,64,2560]{4,3,2,1,0:T(8,128)(2,1)}, bf16[1,1,2,64,2560]{4,3,2,1,0:T(8,128)(2,1)}, s32[1,1,2,27]{3,2,1,0:T(2,128)S(1)}, s32[3,20]{1,0:T(4,128)S(1)}, ...), branch_computations={%region_1.2_spmd, %region_2.3_spmd, %region_3.4_spmd, %region_4.5_... | conditional | bytes 8 | solution.py:515
  3.4 47.0 %branch_0_fun.1 = bf16[128,2560]{1,0:T(8,128)(2,1)S(1)} custom-call(bf16[128,2560]{1,0:T(8,128)(2,1)} %bitcast.36, bf16[128,2560]{1,0:T(8,128)(2,1)} %bitcast.43, bf16[128,2560]{1,0:T(8,128)(2,1)} %bitcast.50, s32[3,20]{1,0:T(4,128)S(1)} %get-tuple-element.157.win_ref, s32[2,27]{1,0:T(2,128)S(1)} %bitcast.71, f32[1]{0:T(128)} %get-tuple-element.288.coef_ref, ...), custom_call_target="tpu_custom_call" | custom-call | tf_op jit(solution)/shard_map/cond/branch_0_fun/pallas_call | solution.py:515
  51.0 0.8 %copy.73 = bf16[1,1,2,64,2560]{4,3,2,1,0:T(8,128)(2,1)} copy(bf16[1,1,2,64,2560]{4,3,2,1,0:T(8,128)(2,1)S(1)} %get-tuple-element.210) | data formatting | bytes 1310720
Async XLA Ops:
  2.7 0.7 %copy-start = (s32[20,3]{0,1:T(4,128)S(1)}, s32[20,3]{0,1:T(4,128)}, u32[]{:S(2)}) copy-start(s32[20,3]{0,1:T(4,128)} %param.18) | copy-start | bytes 724
  2.7 0.7 %copy-start.1 = (s32[1,1,2,27]{3,2,1,0:T(2,128)S(1)}, s32[1,1,2,27]{3,2,1,0:T(2,128)}, u32[]{:S(2)}) copy-start(s32[1,1,2,27]{3,2,1,0:T(2,128)} %param.19) | copy-start | bytes 652

commit v3 on v2

--- a/solution.py
+++ b/solution.py
@@ -12,11 +12,11 @@
 NEG = -1e30
 MESH = pl.DeviceIdType.MESH
 HC = 1
-FULL, CROSS, NEAR = range(3)
+FULL, CROSS, NEAR, SELF = range(4)
 
 
 def kernel(
-    n_tm, n_height, heads, full_chunks, reach_chunks,
+    n_tm, n_height, heads, full_chunks, reach_chunks, row_chunks,
     q_hbm, k_hbm, v_hbm, win_ref, mask_hbm, coef_ref, layer_ref, steer_hbm,
     out_ref,
     kbuf, vbuf, qbuf, mbuf, bias, scores, svec, ostage,
@@ -84,14 +84,22 @@
     both = [along[h] * jnp.where(win_ref[1, h] >= 1, 1, 0) for h in range(heads)]
     n_along = functools.reduce(lambda a, b: a + b, along)
     n_both = functools.reduce(lambda a, b: a + b, both)
-    place_both, place_along, place_rest = jnp.int32(0), n_both, n_along
+    over = [(1 - along[h]) * jnp.where(win_ref[1, h] >= 1, 1, 0) for h in range(heads)]
+    n_over = functools.reduce(lambda a, b: a + b, over)
+    place_both, place_along = jnp.int32(0), n_both
+    place_over, place_rest = n_along, n_along + n_over
     for h in range(heads):
         rank[h] = jnp.where(
-            both[h] == 1, place_both, jnp.where(along[h] == 1, place_along, place_rest)
+            both[h] == 1,
+            place_both,
+            jnp.where(
+                along[h] == 1, place_along, jnp.where(over[h] == 1, place_over, place_rest)
+            ),
         )
         place_both = place_both + both[h]
         place_along = place_along + along[h] - both[h]
-        place_rest = place_rest + 1 - along[h]
+        place_over = place_over + over[h]
+        place_rest = place_rest + 1 - along[h] - over[h]
 
     def invert(i, _):
         head = jnp.int32(0)
@@ -213,7 +221,7 @@
 
     start_rows(0, 0)
     start_frames(0)
-    lax.fori_loop(1, chunks, start_rows, 0)
+    lax.fori_loop(1, row_chunks, start_rows, 0)
     pack(2, q_ref)
     lax.fori_loop(0, chunks, start_local, 0)
     loads[3].wait()
@@ -333,21 +341,22 @@
     def attend(kind, g, _):
         slots = [
             slot for slot in range(ns)
-            if kind == FULL or slot < nr or (kind == CROSS and slot % nr == 0)
+            if slot == 0 or kind == FULL or (slot < nr and kind != SELF)
+            or (kind == CROSS and slot % nr == 0)
         ]
         keep_q(g).wait()
         send_q(g).wait_recv()
         for kv in range(2):
             keep(kv, g).wait()
             arrived(kv, 0, g, sib).wait_recv()
-        if kind != FULL:
+        if kind in (CROSS, NEAR):
             for j in range(nr - 1):
                 def near(j=j):
                     for core in range(2):
                         for kv in range(2):
                             arrived(kv, 1 + j, g, jnp.int32(core)).wait_recv()
                 guard(row_ok(j), near)
-        for i in range(2 if kind != NEAR else 0):
+        for i in range(2 if kind in (FULL, CROSS) else 0):
             def body(i=i):
                 for kv in range(2):
                     for core in range(2):
@@ -400,12 +409,13 @@
         if start < stop:
             lax.fori_loop(start, stop, functools.partial(step, kind), 0)
 
+    run(row_chunks, chunks, attend, SELF)
     if full_chunks == reach_chunks and 2 * full_chunks > chunks:
-        run(reach_chunks, chunks, attend, NEAR)
+        run(reach_chunks, row_chunks, attend, NEAR)
         run(0, full_chunks, attend, FULL)
     else:
         run(0, full_chunks, attend, FULL)
-        run(reach_chunks, chunks, attend, NEAR)
+        run(reach_chunks, row_chunks, attend, NEAR)
         run(full_chunks, reach_chunks, attend, CROSS)
 
     send_mask().wait_send()
@@ -414,13 +424,13 @@
         send_q(g).wait_send()
         for kv in range(2):
             to_sibling(kv, g).wait_send()
-        for i in range(nr - 1):
+        for i in range(nr - 1 if kind != SELF else 0):
             def body(i=i):
                 for core in range(2):
                     for kv in range(2):
                         to_row(kv, i, g, core).wait_send()
             guard(row_ok(i), body)
-        for i in range(2 if kind != NEAR else 0):
+        for i in range(2 if kind in (FULL, CROSS) else 0):
             def body(i=i):
                 for kv in range(2):
                     for core in range(2):
@@ -437,7 +447,8 @@
 
     run(0, full_chunks, drain, FULL)
     run(full_chunks, reach_chunks, drain, CROSS)
-    run(reach_chunks, chunks, drain, NEAR)
+    run(reach_chunks, row_chunks, drain, NEAR)
+    run(row_chunks, chunks, drain, SELF)
 
     for h in range(heads):
         spot = rank[h]
@@ -464,9 +475,9 @@
         offsets = tile_mask.shape[-1]
         packed = pltpu.VMEM((chunks, 2, tokens, cw), bf16)
 
-        def attention(number, full_chunks, reach_chunks):
+        def attention(number, *plan):
             return pl.pallas_call(
-                functools.partial(kernel, n_tm, n_height, heads, full_chunks, reach_chunks),
+                functools.partial(kernel, n_tm, n_height, heads, *plan),
                 out_shape=jax.ShapeDtypeStruct(flat, bf16),
                 in_specs=[hbm, hbm, hbm, smem, hbm, smem, smem, hbm],
                 out_specs=vmem,
@@ -502,15 +513,16 @@
                 ),
             )
 
-        plans = [(5, 5), (4, 6), (4, 7), (6, 6), (5, 8), (7, 7)]
-        plans = [plan for plan in plans if plan[1] < chunks] + [(chunks, chunks)]
+        plans = [(5, 5, 8), (4, 6, 8), (5, 7, 8), (5, 5, 10), (5, 7, 10), (6, 8, 10)]
+        plans = [plan for plan in plans if plan[1] < chunks and plan[2] <= chunks]
+        plans.append((chunks, chunks, chunks))
         along = windows[:, 0] >= 1
-        both = along & (windows[:, 1] >= 1)
-        counts = jnp.sum(along.astype(jnp.int32) * 64 + both.astype(jnp.int32))
-        n_along, n_both = counts >> 6, counts & 63
+        over = windows[:, 1] >= 1
+        counts = jnp.sum(jnp.where(along, 4096, 0) + jnp.where(along & over, 64, 0) + jnp.where(along | over, 1, 0))
+        n_along, n_both, n_either = counts >> 12, (counts >> 6) & 63, counts & 63
         choice = jnp.int32(len(plans) - 1)
-        for n, (full, reach) in reversed(list(enumerate(plans[:-1]))):
-            fits = (n_both <= 2 * HC * full) & (n_along <= 2 * HC * reach)
+        for n, (full, reach, row) in reversed(list(enumerate(plans[:-1]))):
+            fits = (n_both <= 2 * HC * full) & (n_along <= 2 * HC * reach) & (n_either <= 2 * HC * row)
             choice = jnp.where(fits, n, choice)
         out = lax.switch(
             choice,

time: 52 us -> 51.7 us (level)
  Pallas kernels: 47 us -> 46 us
  between operations: 1.36 us -> 2.02 us
    pallas_call x1, Pallas kernels: 47 us -> 46 us  [per_device(): lax.switch(choice, [attention(n, *plan) for n, plan in enumerate(plans)],...]
where the time goes in v3:
time: 51.7 us; the launch traced here: 51.4 us
  Pallas kernels  46 us (89%)
  between operations  2.02 us (4%)
  local copies, waits for them, and re-layouts  1.52 us (3%)
  other arithmetic  1.4 us (3%)
  loops' own time  0.54 us (1%)
    pallas_call x1, Pallas kernels, per_device(): lax.switch(choice, [attention(n, *plan) for n, plan in enumerate(plans)],...  46 us
    unnamed x5, local copies, waits for them, and re-layouts  1.52 us
    reduce_sum x1, other arithmetic, per_device(): jnp.sum(jnp.where(along, 4096, 0) + jnp.where(along & over, 64, 0) + jnp....  1.4 us

profile of v3, /device:TPU:0, one launch (start us, length us, event | category | flops | bytes accessed | tf_op | source)
XLA Modules:
  0.0 51.4 jit_solution(13877743724862308454)
XLA Ops:
  0.0 1.4 %fusion.2 = s32[]{:T(128)} fusion(s32[20,3]{0,1:T(4,128)} %param.18), kind=kLoop, calls=%fused_computation.4 | loop fusion | flops 199 | bytes 164 | tf_op jit(solution)/shard_map/reduce_sum | solution.py:521
  3.4 0.0 copy-start
  3.4 0.0 copy-start.1
  3.4 0.7 %copy-done = s32[20,3]{0,1:T(4,128)S(1)} copy-done((s32[20,3]{0,1:T(4,128)S(1)}, s32[20,3]{0,1:T(4,128)}, u32[]{:S(2)}) %copy-start) | copy-done | bytes 264
  4.1 0.0 copy-done.1
  4.1 46.5 %conditional.1 = (bf16[1,1,2,64,2560]{4,3,2,1,0:T(8,128)(2,1)S(1)}) conditional(s32[]{:T(128)} %clamp.3, (bf16[1,1,2,64,2560]{4,3,2,1,0:T(8,128)(2,1)}, bf16[1,1,2,64,2560]{4,3,2,1,0:T(8,128)(2,1)}, bf16[1,1,2,64,2560]{4,3,2,1,0:T(8,128)(2,1)}, s32[1,1,2,27]{3,2,1,0:T(2,128)S(1)}, s32[3,20]{1,0:T(4,128)S(1)}, ...), branch_computations={%region_1.2_spmd, %region_2.3_spmd, %region_3.4_spmd, %region_4.5_... | conditional | bytes 8 | solution.py:527
  4.1 46.0 %branch_0_fun.1 = bf16[128,2560]{1,0:T(8,128)(2,1)S(1)} custom-call(bf16[128,2560]{1,0:T(8,128)(2,1)} %bitcast.36, bf16[128,2560]{1,0:T(8,128)(2,1)} %bitcast.43, bf16[128,2560]{1,0:T(8,128)(2,1)} %bitcast.50, s32[3,20]{1,0:T(4,128)S(1)} %get-tuple-element.157.win_ref, s32[2,27]{1,0:T(2,128)S(1)} %bitcast.71, f32[1]{0:T(128)} %get-tuple-element.288.coef_ref, ...), custom_call_target="tpu_custom_call" | custom-call | tf_op jit(solution)/shard_map/cond/branch_0_fun/pallas_call | solution.py:527
  50.6 0.8 %copy.73 = bf16[1,1,2,64,2560]{4,3,2,1,0:T(8,128)(2,1)} copy(bf16[1,1,2,64,2560]{4,3,2,1,0:T(8,128)(2,1)S(1)} %get-tuple-element.210) | data formatting | bytes 1310720
Async XLA Ops:
  3.4 0.7 %copy-start = (s32[20,3]{0,1:T(4,128)S(1)}, s32[20,3]{0,1:T(4,128)}, u32[]{:S(2)}) copy-start(s32[20,3]{0,1:T(4,128)} %param.18) | copy-start | bytes 724
  3.4 0.7 %copy-start.1 = (s32[1,1,2,27]{3,2,1,0:T(2,128)S(1)}, s32[1,1,2,27]{3,2,1,0:T(2,128)}, u32[]{:S(2)}) copy-start(s32[1,1,2,27]{3,2,1,0:T(2,128)} %param.19) | copy-start | bytes 652
